TPU v7x, 128 devices: a whole 4x4x4 slice. The times are simulated.
128 devices in a mesh: wide: 32 (over x_hi, y, z), narrow: 4 (over x_lo, core).
Axes of the slice: x: 4 (x_hi: 2, x_lo: 2; x = x_hi * 2 + x_lo), y: 4, z: 4, core: 2. Of those that a mesh axis runs over, the one named last changes fastest.
Arguments:
- jacobian: bfloat16 [32768, 32768], P('wide', 'narrow'), may hold values from -0.03125 to 0.03125
- prior_scale: float32 [32768], P('narrow'), may hold values from 0.5 to 2
- lag_one: float32 [64], replicated, may hold values from 0.2 to 0.8
- lag_two: float32 [64], replicated, may hold values from -0.4 to 0.15
- noise_scale: float32 [64], replicated, may hold values from 0.3 to 3
- sketch_seed: int32 [1], replicated, may hold values from 0 to 1048575
Outputs:
- pulled_back: float32 [512, 32768], P('wide', 'narrow')
All inputs are finite; a program needn't handle non-finite values.
Results may differ from a plain program's by a relative error of at most 0.0038.
Values may be sent and summed in bfloat16 or wider, within the bound.
A program may use at most 128 MiB of HBM per device.

v0:
```python
import jax
import jax.numpy as jnp
from jax import lax
from jax.sharding import PartitionSpec as P

K = 512
S = 64


def sketch_table(seed_value, row_count, first_row):
    param_index = (first_row + jnp.arange(row_count, dtype=jnp.int32))[:, None]
    column_index = jnp.arange(K, dtype=jnp.int32)[None, :]
    hashed = param_index * K + column_index
    hashed = hashed ^ seed_value[0] * 747796405
    hashed = hashed * -1640531535
    hashed = hashed ^ hashed >> 15 & 131071
    hashed = hashed * 739982445
    hashed = hashed ^ hashed >> 12 & 1048575
    hashed = hashed * 695872825
    hashed = hashed ^ hashed >> 15 & 131071
    uniform = (hashed >> 8 & 16777215).astype(jnp.float32) * (1.0 / 16777216.0)
    return 1.7320508 * (2.0 * uniform - 1.0)


def whiten_forward(values, lag_one, lag_two, noise_scale):
    prev_one = jnp.pad(values, ((1, 0), (0, 0), (0, 0)))[:-1]
    prev_two = jnp.pad(values, ((2, 0), (0, 0), (0, 0)))[:-2]
    return (values - lag_one[:, None] * prev_one - lag_two[:, None] * prev_two) / noise_scale[
        :, None
    ]


def whiten_adjoint(values, lag_one, lag_two, noise_scale):
    next_one = jnp.pad(values, ((0, 1), (0, 0), (0, 0)))[1:]
    next_two = jnp.pad(values, ((0, 2), (0, 0), (0, 0)))[2:]
    return (values - lag_one[:, None] * next_one - lag_two[:, None] * next_two) / noise_scale[
        :, None
    ]


def whiten_both(images, lag_one, lag_two, noise_scale):
    records = lax.all_to_all(images, "wide", split_axis=1, concat_axis=0, tiled=True)
    count_here = records.shape[1]
    first_sensor = lax.axis_index("wide") * count_here
    local_one = lax.dynamic_slice_in_dim(lag_one, first_sensor, count_here)
    local_two = lax.dynamic_slice_in_dim(lag_two, first_sensor, count_here)
    local_scale = lax.dynamic_slice_in_dim(noise_scale, first_sensor, count_here)
    forward = whiten_forward(records, local_one, local_two, local_scale)
    adjoint = whiten_adjoint(forward, local_one, local_two, local_scale).astype(jnp.bfloat16)
    return lax.all_to_all(adjoint, "wide", split_axis=0, concat_axis=1, tiled=True)


def shards(jacobian, prior_scale, lag_one, lag_two, noise_scale, sketch_seed):
    row_count, tile_width = jacobian.shape
    time_steps = row_count // S
    first_param = lax.axis_index("narrow") * tile_width
    sketch = (prior_scale[:, None] * sketch_table(sketch_seed, tile_width, first_param)).astype(
        jnp.bfloat16
    )
    partial_images = jnp.dot(jacobian, sketch, preferred_element_type=jnp.float32)
    images = lax.psum(partial_images, "narrow")
    columns = images.shape[1]
    adjoint = whiten_both(images.reshape(time_steps, S, columns), lag_one, lag_two, noise_scale)
    adjoint = adjoint.reshape(row_count, columns)
    product = lax.psum_scatter(
        lax.dot_general(
            adjoint, jacobian, (((0,), (0,)), ((), ())), preferred_element_type=jnp.float32
        ),
        "wide",
        scatter_dimension=0,
        tiled=True,
    )
    return product * prior_scale[None, :]


def solution(mesh):
    in_specs = (P("wide", "narrow"), P("narrow"), P(), P(), P(), P())
    out_specs = P("wide", "narrow")
    return jax.shard_map(shards, mesh=mesh, in_specs=in_specs, out_specs=out_specs, check_vma=False)
```

profile of v0, /device:TPU:0, one launch (start us, length us, event | category | flops | bytes accessed | tf_op | source)
XLA Modules:
  0.0 412.6 jit_solution(10102495621289084355)
XLA Ops:
  6.5 0.0 all-reduce.6.cloned.1.call-start
  7.2 0.8 broadcast_multiply_fusion.1
  8.0 0.0 copy-start.1
  8.0 0.0 copy-start.2
  8.0 0.0 copy-start.3
  8.0 24.0 %fusion.26 = f32[1024,512]{0,1:T(8,128)S(1)} fusion(bf16[1024,8192]{1,0:T(8,128)(2,1)} %param.6, f32[8192]{0:T(1024)S(1)} %broadcast_multiply_fusion.1, s32[]{:T(128)} %bitcast, s32[8192]{0:T(1024)S(1)} %add_multiply_fusion), kind=kOutput, calls=%fused_computation.31 | convolution fusion | flops 8678014976 | bytes 18939908 | tf_op jit(solution)/shard_map/dot_general | solution.py:60
  32.0 1.8 copy.11
  33.8 0.0 all-reduce.6.cloned.1.call-update
  33.9 59.7 %all-reduce.6.cloned.1.call-done = f32[16,64,512]{2,1,0:T(8,128)} async-done(((f32[16,64,512]{2,1,0:T(8,128)}), f32[16,64,512]{2,1,0:T(8,128)}) %all-reduce.6.cloned.1.call-update) | async-done | bytes 2097168 | tf_op jit(solution)/shard_map/psum | solution.py:61
  93.6 4.1 copy.12
  97.7 9.4 %all-to-all-start = ((f32[16,64,512]{2,0,1:T(8,128)}), f32[16,64,512]{2,0,1:T(8,128)S(1)}, u32[]{:S(2)}, u32[]{:S(2)}) async-start(f32[16,64,512]{2,0,1:T(8,128)} %copy.12), calls=%async_computation | async-start | bytes 4194304 | tf_op jit(solution)/shard_map/all_to_all | solution.py:42
  107.1 0.0 reduce-scatter.2.cloned.1.call-start
  107.2 0.0 copy-done.1
  107.2 0.1 dynamic_slice.9
  107.2 0.0 copy-done.2
  107.2 0.1 dynamic_slice.10
  107.3 0.0 copy-done.3
  107.3 0.1 dynamic_slice.11
  107.4 28.7 %all-to-all-done = f32[16,64,512]{2,0,1:T(8,128)S(1)} async-done(((f32[16,64,512]{2,0,1:T(8,128)}), f32[16,64,512]{2,0,1:T(8,128)S(1)}, u32[]{:S(2)}, u32[]{:S(2)}) %all-to-all-start) | async-done | bytes 2097184 | tf_op jit(solution)/shard_map/all_to_all | solution.py:42
  136.1 0.3 copy.13
  136.4 0.7 fusion.18
  137.1 0.7 fusion.25
  137.8 1.1 copy.14
  138.9 24.9 %all_to_all.33 = bf16[512,2,512]{2,1,0:T(2,128)(2,1)S(1)} all-to-all(bf16[512,2,512]{2,1,0:T(2,128)(2,1)S(1)} %copy.14), channel_id=1, replica_groups=mesh['wide'=32,'narrow'=4] {'wide'}, dimensions={0} | all-to-all | bytes 2097152 | tf_op jit(solution)/shard_map/all_to_all | solution.py:50
  163.8 1.0 copy.17
  164.7 0.4 reshape.21
  165.2 15.9 %fusion.38 = f32[512,8192]{1,0:T(8,128)} fusion(bf16[1024,512]{1,0:T(8,128)(2,1)S(1)} %reshape.21, bf16[1024,8192]{1,0:T(8,128)(2,1)} %param.6), kind=kOutput, calls=%fused_computation.47 | convolution fusion | flops 8589934592 | bytes 34603008 | tf_op jit(solution)/shard_map/dot_general | solution.py:66
  181.0 0.0 copy-start
  181.0 0.0 reduce-scatter.2.cloned.1.call-update
  181.1 222.9 %reduce-scatter.2.cloned.1.call-done = f32[16,8192]{1,0:T(8,128)} async-done(((f32[512,8192]{1,0:T(8,128)}), f32[16,8192]{1,0:T(8,128)}) %reduce-scatter.2.cloned.1.call-update) | async-done | bytes 524304 | tf_op jit(solution)/shard_map/reduce_scatter | solution.py:65
  403.9 0.0 copy-done
  403.9 1.9 broadcast_multiply_fusion
  (1 shorter events, 0.0 us)
Async XLA Ops:
  6.5 87.1 %all-reduce.6.cloned.1.call-start = ((), (), s32[]{:S(2)}) async-start(), calls=%async_computation.3 | async-start | bytes 4194304 | tf_op jit(solution)/shard_map/psum | solution.py:61
  8.0 99.2 %copy-start.1 = (f32[64]{0:T(128)S(1)}, f32[64]{0:T(128)}, u32[]{:S(2)}) copy-start(f32[64]{0:T(128)} %param.8) | copy-start | bytes 772
  8.0 99.3 %copy-start.2 = (f32[64]{0:T(128)S(1)}, f32[64]{0:T(128)}, u32[]{:S(2)}) copy-start(f32[64]{0:T(128)} %param.9) | copy-start | bytes 772
  8.0 99.4 %copy-start.3 = (f32[64]{0:T(128)S(1)}, f32[64]{0:T(128)}, u32[]{:S(2)}) copy-start(f32[64]{0:T(128)} %param.10) | copy-start | bytes 772
  97.7 38.4 %all-to-all-start = ((f32[16,64,512]{2,0,1:T(8,128)}), f32[16,64,512]{2,0,1:T(8,128)S(1)}, u32[]{:S(2)}, u32[]{:S(2)}) async-start(f32[16,64,512]{2,0,1:T(8,128)} %copy.12), calls=%async_computation | async-start | bytes 4194304 | tf_op jit(solution)/shard_map/all_to_all | solution.py:42
  107.1 296.8 %reduce-scatter.2.cloned.1.call-start = ((), (), s32[]{:S(2)}) async-start(), calls=%async_computation.4 | async-start | bytes 17301504 | tf_op jit(solution)/shard_map/reduce_scatter | solution.py:65
  181.0 222.9 %copy-start = (f32[8192]{0:T(1024)S(1)}, f32[8192]{0:T(1024)}, u32[]{:S(2)}) copy-start(f32[8192]{0:T(1024)} %param.7) | copy-start | bytes 98308
Sparse Core Ops, SparseCore 0:
  34.0 59.5 all-reduce.5
  181.2 222.6 reduce-scatter.1
where the time goes:
time: 413 us
  waiting for transfers between devices  311 us (75%)
  matrix products  39.9 us (10%)
  blocking collectives  24.9 us (6%)
  between operations  14.1 us (3%)
  starting transfers between devices  9.43 us (2%)
  local copies, waits for them, and re-layouts  8.97 us (2%)
    reduce_scatter x1, waiting for transfers between devices, shards(): lax.psum_scatter(lax.dot_general(adjoint, jacobian, (((0,), (0,)), ((), (...  223 us
    psum x1, waiting for transfers between devices, shards(): images = lax.psum(partial_images, 'narrow')  59.7 us
    all_to_all x1, waiting for transfers between devices, whiten_both(): lax.all_to_all(images, 'wide', split_axis=1, concat_axis=0, tiled=True)  28.7 us
    all_to_all x1, blocking collectives, whiten_both(): lax.all_to_all(adjoint, 'wide', split_axis=0, concat_axis=1, tiled=True)  24.9 us
    dot_general x1, matrix products, shards(): jnp.dot(jacobian, sketch, preferred_element_type=jnp.float32)  24 us
    dot_general x1, matrix products, shards(): lax.dot_general(adjoint, jacobian, (((0,), (0,)), ((), ())), preferred_el...  15.9 us
    all_to_all x1, starting transfers between devices, whiten_both(): lax.all_to_all(images, 'wide', split_axis=1, concat_axis=0, tiled=True)  9.39 us
  transfers between devices with their start and end apart: 3, of which 3 were waited for; matrix products, arithmetic and copies ran while one was open for 0% of the time, Pallas kernels for 0%

commit v1 on v0

v1 whole, which is shorter than its diff:
```python
import functools

import jax
import jax.numpy as jnp
import numpy as np
from jax import lax
from jax.experimental import pallas as pl
from jax.experimental.pallas import tpu as pltpu
from jax.sharding import PartitionSpec as P

K = 512
S = 64
MESH = pl.DeviceIdType.MESH
CW = 512
HW = CW // 2
GW = 1024
M1, M2, M3 = -1640531535, 739982445, 695872825
SPREAD = float(np.float32(1.7320508) * np.float32(2.0**-23))


def kernel(
    j_hbm, prior, coef, seed, out,
    jbuf, sk0, sk1, acc, rxc, rxx, img, halo, adj,
    s_buf, r1opp, r1raw, r1sum, f1, t_f32, t_b16, r2opp, r2raw, r2sum, f2, u_f32, u_b16, r3,
    j_sem, a_send, a_recv, b_send, b_recv,
):
    n_chunks = jbuf.shape[0]
    rows = jbuf.shape[1]
    width = n_chunks * CW
    wide, narrow = lax.axis_index("wide"), lax.axis_index("narrow")
    xh, y, z = wide // 16, (wide // 4) % 4, wide % 4
    xl, core = narrow // 2, narrow % 2
    at = lambda w: (w, narrow)
    mate = (wide, xl * 2 + (1 - core))
    across = (wide, (1 - xl) * 2 + core)
    later, earlier = at((wide + 1) % 32), at((wide + 31) % 32)
    rights = (at(xh * 16 + ((y + 1) % 4) * 4 + z), at(xh * 16 + y * 4 + (z + 1) % 4))
    lefts = (at(xh * 16 + ((y + 3) % 4) * 4 + z), at(xh * 16 + y * 4 + (z + 3) % 4))
    xmate = at((1 - xh) * 16 + y * 4 + z)

    def load(c):
        return pltpu.make_async_copy(
            j_hbm.at[:, pl.ds(pl.multiple_of(c * CW, CW), CW)], jbuf.at[c], j_sem.at[c]
        )

    @pl.loop(0, n_chunks)
    def _(c):
        load(c).start()

    barrier = pltpu.get_barrier_semaphore()
    partners = (mate, across, later, earlier, *rights, *lefts, xmate)
    for partner in partners:
        pl.semaphore_signal(barrier, inc=1, device_id=partner, device_id_type=MESH)

    salt = seed[0] * 747796405
    salt_high, salt_low = salt & -512, salt & 511

    def generate(g, dest):
        first = narrow * width + g * GW
        across_p = (
            ((lax.broadcasted_iota(jnp.int32, (16, GW), 1) + first) * 512) ^ salt_high
        ) * M1
        scale = jnp.broadcast_to(prior[:, pl.ds(pl.multiple_of(g * GW, GW), GW)], (16, GW))
        for block in range(K // 16):
            down = lax.broadcasted_iota(jnp.int32, (16, 128), 0) + block * 16
            down = (down ^ salt_low) * M1
            h = across_p + jnp.concatenate([down] * (GW // 128), axis=1)
            h = h ^ lax.shift_right_logical(h, 15)
            h = h * M2
            h = h ^ lax.shift_right_logical(h, 12)
            h = h * M3
            h = h ^ lax.shift_right_logical(h, 15)
            h = lax.shift_right_logical(h, 8) - 8388608
            omega = h.astype(jnp.float32) * SPREAD
            dest[block * 16 : block * 16 + 16, :] = (scale * omega).astype(jnp.bfloat16)

    def multiply(g, source):
        total = acc[...].reshape(K, rows)
        for part in range(GW // CW):
            load(g * (GW // CW) + part).wait()
            total += lax.dot_general(
                source[:, part * CW : part * CW + CW],
                jbuf[g * (GW // CW) + part],
                (((1,), (1,)), ((), ())),
                preferred_element_type=jnp.float32,
            )
        acc[...] = total.reshape(acc.shape)

    acc[...] = jnp.zeros_like(acc)
    generate(0, sk0)
    n_gen = width // GW

    @pl.loop(0, n_gen // 2)
    def _(i):
        multiply(2 * i, sk0)
        generate(2 * i + 1, sk1)
        multiply(2 * i + 1, sk1)
        generate((2 * i + 2) % n_gen, sk0)

    pl.semaphore_wait(barrier, len(partners))

    def to_mate(slot):
        x = (1 - xl) if slot == 0 else xl
        return pltpu.make_async_remote_copy(
            acc.at[x * 2 + (1 - core)], rxc.at[slot], a_send.at[slot], a_recv.at[slot],
            device_id=mate, device_id_type=MESH,
        )

    edges = ((0, 128), (rows - 128, rows), (128, rows - 128))

    def to_across(piece):
        low, high = edges[piece]
        return pltpu.make_async_remote_copy(
            rxx.at[1, :, low:high], rxx.at[0, :, low:high],
            a_send.at[2 + piece], a_recv.at[2 + piece],
            device_id=across, device_id_type=MESH,
        )

    def to_time(side):
        src = img.at[:, 128:256] if side == 0 else img.at[:, rows : rows + 128]
        return pltpu.make_async_remote_copy(
            src, halo.at[side], a_send.at[5 + side], a_recv.at[5 + side],
            device_id=earlier if side == 0 else later, device_id_type=MESH,
        )

    to_mate(0).start()
    to_mate(1).start()
    to_mate(0).wait_recv()
    rxx[1] = acc[(1 - xl) * 2 + core] + rxc[0]
    for piece in range(3):
        to_across(piece).start()
    to_mate(1).wait_recv()
    rxc[1] = acc[xl * 2 + core] + rxc[1]
    for piece in range(3):
        low, high = edges[piece]
        to_across(piece).wait_recv()
        img[:, 128 + low : 128 + high] = rxc[1, :, low:high] + rxx[0, :, low:high]
        if piece < 2:
            to_time(piece).start()
    to_time(0).wait_recv()
    to_time(1).wait_recv()
    to_time(0).wait_send()
    to_time(1).wait_send()
    img[:, rows + 128 :] = halo[0]
    img[:, :128] = jnp.where(wide == 0, jnp.zeros((128, 128), jnp.float32), halo[1])

    whole = rows + 256
    reps = whole // 128
    spread = lambda i: jnp.concatenate([jnp.broadcast_to(coef[i : i + 1, :], (32, 128))] * reps, axis=1)
    lag_one, lag_two, scale = spread(0), spread(1), spread(2)
    lane = lax.broadcasted_iota(jnp.int32, (32, whole), 1)
    limit = jnp.where(wide == 31, rows + 128, whole)
    mine = xl * 2 + core
    for block in range(4):
        part = slice(block * 32, block * 32 + 32)
        v = img[part, :]
        w = (v - lag_one * pltpu.roll(v, S, 1) - lag_two * pltpu.roll(v, 2 * S, 1)) / scale
        w = jnp.where(lane < limit, w, 0.0)
        a = (
            w - lag_one * pltpu.roll(w, whole - S, 1) - lag_two * pltpu.roll(w, whole - 2 * S, 1)
        ) / scale
        adj[mine, part, :] = a[:, 128 : 128 + rows].astype(jnp.bfloat16)

    def share(which):
        q = mine if which < 2 else (1 - xl) * 2 + core
        return pltpu.make_async_remote_copy(
            adj.at[q], adj.at[q], a_send.at[7 + which], a_recv.at[7 + which],
            device_id=across if which == 0 else mate, device_id_type=MESH,
        )

    share(0).start()
    share(1).start()
    share(0).wait_recv()
    share(2).start()
    share(1).wait_recv()
    share(2).wait_recv()

    def remote(c, kind, src, dst, device):
        return pltpu.make_async_remote_copy(
            src, dst, b_send.at[c, kind], b_recv.at[c, kind],
            device_id=device, device_id_type=MESH,
        )

    def place(color):
        return (y, z) if color == 0 else (z, y)

    def own(color, c, h, j):
        return s_buf.at[c, h, :, j] if color == 0 else s_buf.at[c, h, :, :, j]

    def first(color, c, kind):
        d = place(color)[0]
        right, left = rights[color], lefts[color]
        if kind == 0:
            return remote(c, 0, own(color, c, 0, (d + 2) % 4), r1opp.at[c, 0], right)
        if kind == 1:
            return remote(c, 1, own(color, c, 1, (d + 2) % 4), r1opp.at[c, 1], left)
        if kind == 2:
            return remote(c, 2, own(color, c, 1, (d + 1) % 4), r1raw.at[c, 0], right)
        if kind == 3:
            return remote(c, 3, own(color, c, 0, (d + 3) % 4), r1raw.at[c, 1], left)
        if kind == 4:
            return remote(c, 4, f1.at[c, 0], r1sum.at[c, 0], right)
        return remote(c, 5, f1.at[c, 1], r1sum.at[c, 1], left)

    def second(color, c, kind):
        d = place(color)[1]
        right, left = rights[1 - color], lefts[1 - color]
        if kind == 0:
            return remote(c, 6, t_b16.at[c, 0, :, (d + 2) % 4], r2opp.at[c, 0], right)
        if kind == 1:
            return remote(c, 7, t_b16.at[c, 1, :, (d + 2) % 4], r2opp.at[c, 1], left)
        if kind == 2:
            return remote(c, 8, t_b16.at[c, 1, :, (d + 1) % 4], r2raw.at[c, 0], right)
        if kind == 3:
            return remote(c, 9, t_b16.at[c, 0, :, (d + 3) % 4], r2raw.at[c, 1], left)
        if kind == 4:
            return remote(c, 10, f2.at[c, 0], r2sum.at[c, 0], right)
        return remote(c, 11, f2.at[c, 1], r2sum.at[c, 1], left)

    def third(c):
        return remote(c, 12, u_b16.at[c, 1 - xh], r3.at[c], xmate)

    f32 = lambda v: v.astype(jnp.float32)

    def product(color, c):
        lhs = adj[...].reshape(K, rows)
        for h in range(2):
            value = jnp.dot(
                lhs, jbuf[c, :, h * HW : h * HW + HW], preferred_element_type=jnp.float32
            )
            s_buf[c, h] = value.astype(jnp.bfloat16).reshape(s_buf.shape[2:])
        for kind in range(4):
            first(color, c, kind).start()

    def relay_one(color, c):
        d = place(color)[0]
        for side in range(2):
            first(color, c, side).wait_recv()
            mine_ref = own(color, c, side, (d + (1 if side == 0 else 3)) % 4)
            f1[c, side] = (f32(r1opp[c, side]) + f32(mine_ref[...])).astype(jnp.bfloat16)
            first(color, c, 4 + side).start()

    def finish_one(color, c):
        d = place(color)[0]
        for kind in range(2, 6):
            first(color, c, kind).wait_recv()
        for h in range(2):
            value = f32(own(color, c, h, d)[...]) + f32(r1sum[c, h]) + f32(r1raw[c, 1 - h])
            t_f32[c, h] = value
            t_b16[c, h] = value.astype(jnp.bfloat16)
        for kind in range(4):
            second(color, c, kind).start()

    def relay_two(color, c):
        d = place(color)[1]
        for side in range(2):
            second(color, c, side).wait_recv()
            value = f32(r2opp[c, side]) + t_f32[c, side, :, (d + (1 if side == 0 else 3)) % 4]
            f2[c, side] = value.astype(jnp.bfloat16)
            second(color, c, 4 + side).start()

    def finish_two(color, c):
        d = place(color)[1]
        for kind in range(2, 6):
            second(color, c, kind).wait_recv()
        for h in range(2):
            value = t_f32[c, h, :, d] + f32(r2sum[c, h]) + f32(r2raw[c, 1 - h])
            for x in range(2):
                u_f32[c, x, h] = value[x]
                u_b16[c, x, h] = value[x].astype(jnp.bfloat16)
        third(c).start()

    def finish(color, c):
        third(c).wait_recv()
        for h in range(2):
            lanes = pl.ds(pl.multiple_of(c * CW + h * HW, HW), HW)
            out[:, lanes] = u_f32[c, xh, h] + f32(r3[c, h])

    stages = (product, relay_one, finish_one, relay_two, finish_two, finish)
    n_rounds = n_chunks // 2

    @pl.loop(0, n_rounds + len(stages) - 1)
    def _(i):
        for lag, stage in enumerate(stages):

            @pl.when((i >= lag) & (i < n_rounds + lag))
            def _():
                for color in range(2):
                    stage(color, 2 * (i - lag) + color)

    to_mate(0).wait_send()
    to_mate(1).wait_send()
    for piece in range(3):
        to_across(piece).wait_send()
    for which in range(3):
        share(which).wait_send()

    @pl.loop(0, n_rounds)
    def _(i):
        for color in range(2):
            c = 2 * i + color
            for kind in range(6):
                first(color, c, kind).wait_send()
                second(color, c, kind).wait_send()
            third(c).wait_send()


def shards(jacobian, prior_scale, lag_one, lag_two, noise_scale, sketch_seed):
    rows, width = jacobian.shape
    n = width // CW
    coef = jnp.stack([lag_one, lag_two, noise_scale])
    coef = jnp.concatenate([coef, coef], axis=1)
    bf16, f32 = jnp.bfloat16, jnp.float32
    vmem = pl.BlockSpec(memory_space=pltpu.VMEM)
    product = pl.pallas_call(
        kernel,
        out_shape=jax.ShapeDtypeStruct((K // 32, width), f32),
        in_specs=[
            pl.BlockSpec(memory_space=pl.ANY), vmem, vmem, pl.BlockSpec(memory_space=pltpu.SMEM),
        ],
        out_specs=vmem,
        scratch_shapes=[
            pltpu.VMEM((n, rows, CW), bf16),
            pltpu.VMEM((K, GW), bf16),
            pltpu.VMEM((K, GW), bf16),
            pltpu.VMEM((4, K // 4, rows), f32),
            pltpu.VMEM((2, K // 4, rows), f32),
            pltpu.VMEM((2, K // 4, rows), f32),
            pltpu.VMEM((K // 4, rows + 256), f32),
            pltpu.VMEM((2, K // 4, 128), f32),
            pltpu.VMEM((4, K // 4, rows), bf16),
            pltpu.VMEM((n, 2, 2, 4, 4, 16, HW), bf16),
            pltpu.VMEM((n, 2, 2, 4, 16, HW), bf16),
            pltpu.VMEM((n, 2, 2, 4, 16, HW), bf16),
            pltpu.VMEM((n, 2, 2, 4, 16, HW), bf16),
            pltpu.VMEM((n, 2, 2, 4, 16, HW), bf16),
            pltpu.VMEM((n, 2, 2, 4, 16, HW), f32),
            pltpu.VMEM((n, 2, 2, 4, 16, HW), bf16),
            pltpu.VMEM((n, 2, 2, 16, HW), bf16),
            pltpu.VMEM((n, 2, 2, 16, HW), bf16),
            pltpu.VMEM((n, 2, 2, 16, HW), bf16),
            pltpu.VMEM((n, 2, 2, 16, HW), bf16),
            pltpu.VMEM((n, 2, 2, 16, HW), f32),
            pltpu.VMEM((n, 2, 2, 16, HW), bf16),
            pltpu.VMEM((n, 2, 16, HW), bf16),
            pltpu.SemaphoreType.DMA((n,)),
            pltpu.SemaphoreType.DMA((10,)),
            pltpu.SemaphoreType.DMA((10,)),
            pltpu.SemaphoreType.DMA((n, 13)),
            pltpu.SemaphoreType.DMA((n, 13)),
        ],
        compiler_params=pltpu.CompilerParams(
            collective_id=0, has_side_effects=True, vmem_limit_bytes=63 * 1024 * 1024
        ),
    )(jacobian, prior_scale.reshape(1, width), coef, sketch_seed)
    return product * prior_scale[None, :]


def solution(mesh):
    in_specs = (P("wide", "narrow"), P("narrow"), P(), P(), P(), P())
    out_specs = P("wide", "narrow")
    return jax.shard_map(shards, mesh=mesh, in_specs=in_specs, out_specs=out_specs, check_vma=False)
```

time: 413 us -> 117 us (0.28)
  waiting for transfers between devices: 311 us -> 0 us
  Pallas kernels: 0 us -> 113 us
  matrix products: 39.9 us -> 0 us
  blocking collectives: 24.9 us -> 0 us
  between operations: 14.1 us -> 0.68 us
  starting transfers between devices: 9.43 us -> 0 us
  local copies, waits for them, and re-layouts: 8.97 us -> 0.01 us
    reduce_scatter x1 -> x0, waiting for transfers between devices: 223 us -> none  [shards(): lax.psum_scatter(lax.dot_general(adjoint, jacobian, (((0,), (0,)), ((), (...]
    pallas_call x0 -> x1, Pallas kernels: none -> 113 us  [shards(): pl.pallas_call(kernel, out_shape=jax.ShapeDtypeStruct((K // 32, width), f...]
    psum x1 -> x0, waiting for transfers between devices: 59.7 us -> none  [shards(): images = lax.psum(partial_images, 'narrow')]
    dot_general x2 -> x0, matrix products: 39.9 us -> none  [the longest x1 24 us: shards(): jnp.dot(jacobian, sketch, preferred_element_type=jnp.float32)]
    all_to_all x1 -> x0, waiting for transfers between devices: 28.7 us -> none  [whiten_both(): lax.all_to_all(images, 'wide', split_axis=1, concat_axis=0, tiled=True)]
    all_to_all x1 -> x0, blocking collectives: 24.9 us -> none  [whiten_both(): lax.all_to_all(adjoint, 'wide', split_axis=0, concat_axis=1, tiled=True)]
    all_to_all x1 -> x0, starting transfers between devices: 9.39 us -> none  [whiten_both(): lax.all_to_all(images, 'wide', split_axis=1, concat_axis=0, tiled=True)]
  transfers between devices with their start and end apart: 3 -> 0, of which waited for: 3 -> 0; matrix products, arithmetic and copies ran while one was open for 0% -> 0% of each run, Pallas kernels for 0% -> 0%
where the time goes in v1:
time: 117 us
  Pallas kernels  113 us (97%)
  other arithmetic  3.27 us (3%)
    pallas_call x1, Pallas kernels, shards(): pl.pallas_call(kernel, out_shape=jax.ShapeDtypeStruct((K // 32, width), f...  113 us

profile of v1, /device:TPU:0, one launch (start us, length us, event | category | flops | bytes accessed | tf_op | source)
XLA Modules:
  0.0 116.8 jit_solution(453155991389652203)
XLA Ops:
  0.0 0.0 copy-start
  0.7 1.4 %maximum_maximum_fusion.coef = f32[3,128]{1,0:T(4,128)} fusion(f32[1,64]{1,0:T(1,128)} %bitcast.5, f32[1,64]{1,0:T(1,128)} %bitcast.6, f32[1,64]{1,0:T(1,128)} %bitcast.7), kind=kLoop, calls=%fused_computation.1 | loop fusion | flops 1920 | bytes 2304 | tf_op jit(solution)/shard_map/concatenate | solution.py:312
  2.1 112.8 %shard_map.64 = f32[16,8192]{1,0:T(8,128)} custom-call(bf16[1024,8192]{1,0:T(8,128)(2,1)} %j_hbm.1, f32[1,8192]{1,0:T(1,128)} %bitcast.4, f32[3,128]{1,0:T(4,128)} %maximum_maximum_fusion.coef, s32[1]{0:T(128)S(6)} %copy.7.seed), custom_call_target="tpu_custom_call" | custom-call | tf_op jit(solution)/shard_map/pallas_call | solution.py:315
  114.9 0.0 copy-done
  114.9 1.9 %broadcast_multiply_fusion = f32[16,8192]{1,0:T(8,128)} fusion(f32[16,8192]{1,0:T(8,128)} %shard_map.64, f32[8192]{0:T(1024)S(1)} %copy-done), kind=kLoop, calls=%fused_computation | loop fusion | flops 131072 | bytes 1081344 | tf_op jit(solution)/shard_map/mul | solution.py:356
Async XLA Ops:
  0.0 114.9 %copy-start = (f32[8192]{0:T(1024)S(1)}, f32[8192]{0:T(1024)}, u32[]{:S(2)}) copy-start(f32[8192]{0:T(1024)} %param.7) | copy-start | bytes 98308

commit v2 on v0

v2 whole, which is shorter than its diff:
```python
import functools

import jax
import jax.numpy as jnp
import numpy as np
from jax import lax
from jax.experimental import pallas as pl
from jax.experimental.pallas import tpu as pltpu
from jax.sharding import PartitionSpec as P

K = 512
S = 64
MESH = pl.DeviceIdType.MESH
CW = 1024
HW = CW // 2
BLOCK = 256
KH = K // 2
Q = KH // 4
M1, M2, M3 = -1640531535, 739982445, 695872825
SPREAD = float(np.float32(1.7320508) * np.float32(2.0**-23))


def kernel(
    j_hbm, prior, lag_one_in, lag_two_in, scale_in, seed, out,
    jbuf, sk, acc, rxc, rxx, img, halo, adj,
    s_buf, r1opp, r1in, f1, t_f32, t_b16, r2opp, r2in, f2, u_f32, u_b16, r3,
    j_sem, a_send, a_recv, b_send, b_recv,
):
    rows, width = jbuf.shape
    n_chunks = width // CW
    wide, narrow = lax.axis_index("wide"), lax.axis_index("narrow")
    xh, y, z = wide // 16, (wide // 4) % 4, wide % 4
    xl, core = narrow // 2, narrow % 2
    at = lambda w: (w, narrow)
    mate = (wide, xl * 2 + (1 - core))
    across = (wide, (1 - xl) * 2 + core)
    later, earlier = at((wide + 1) % 32), at((wide + 31) % 32)
    rights = (at(xh * 16 + ((y + 1) % 4) * 4 + z), at(xh * 16 + y * 4 + (z + 1) % 4))
    lefts = (at(xh * 16 + ((y + 3) % 4) * 4 + z), at(xh * 16 + y * 4 + (z + 3) % 4))
    xmate = at((1 - xh) * 16 + y * 4 + z)

    def load(b):
        part = pl.ds(pl.multiple_of(b * BLOCK, BLOCK), BLOCK)
        return pltpu.make_async_copy(j_hbm.at[part], jbuf.at[part], j_sem.at[b])

    for b in (3, 0, 1, 2):
        load(b).start()

    barrier = pltpu.get_barrier_semaphore()
    partners = (mate, across, later, earlier, *rights, *lefts, xmate)
    for partner in partners:
        pl.semaphore_signal(barrier, inc=1, device_id=partner, device_id_type=MESH)

    salt = seed[0] * 747796405
    salt_high, salt_low = salt & -512, salt & 511

    def generate(half, g):
        first = narrow * width + g * CW
        lanes = pl.ds(pl.multiple_of(g * CW, CW), CW)
        across_p = (
            ((lax.broadcasted_iota(jnp.int32, (16, CW), 1) + first) * 512) ^ salt_high
        ) * M1
        scale = jnp.broadcast_to(prior[:, lanes] * SPREAD, (16, CW))
        for block in range(KH // 16):
            down = lax.broadcasted_iota(jnp.int32, (16, 128), 0) + (half * KH + block * 16)
            down = (down ^ salt_low) * M1
            h = across_p + jnp.concatenate([down] * (CW // 128), axis=1)
            h = h ^ lax.shift_right_logical(h, 15)
            h = h * M2
            h = h ^ lax.shift_right_logical(h, 12)
            h = h * M3
            h = h ^ lax.shift_right_logical(h, 15)
            h = lax.shift_right_logical(h, 8) - 8388608
            sk[block * 16 : block * 16 + 16, lanes] = (scale * h.astype(jnp.float32)).astype(
                jnp.bfloat16
            )

    def multiply(half, b):
        value = lax.dot_general(
            sk[...], jbuf[pl.ds(pl.multiple_of(b * BLOCK, BLOCK), BLOCK), :],
            (((1,), (1,)), ((), ())), preferred_element_type=jnp.float32,
        )
        acc[half, b] = value.reshape(acc.shape[2:])
        to_mate(half, b).start()

    def to_mate(half, b):
        return pltpu.make_async_remote_copy(
            acc.at[half, b, :, 1 - core], rxc.at[half, b],
            a_send.at[half, b], a_recv.at[half, b],
            device_id=mate, device_id_type=MESH,
        )

    def to_across(half, b):
        return pltpu.make_async_remote_copy(
            rxx.at[half, 1, b], rxx.at[half, 0, b],
            a_send.at[half, 4 + b], a_recv.at[half, 4 + b],
            device_id=across, device_id_type=MESH,
        )

    def to_time(half, side):
        low = 128 if side == 0 else rows
        return pltpu.make_async_remote_copy(
            img.at[half, :, low : low + 128], halo.at[half, side],
            a_send.at[half, 8 + side], a_recv.at[half, 8 + side],
            device_id=earlier if side == 0 else later, device_id_type=MESH,
        )

    mine = xl * 2 + core

    def share(half, which):
        q = mine if which < 2 else (1 - xl) * 2 + core
        return pltpu.make_async_remote_copy(
            adj.at[half, q], adj.at[half, q], a_send.at[half, 10 + which], a_recv.at[half, 10 + which],
            device_id=across if which == 0 else mate, device_id_type=MESH,
        )

    def sum_cores(half, b):
        to_mate(half, b).wait_recv()
        rxx[half, 1, b] = acc[half, b, 1 - xl, core] + rxc[half, b, 1 - xl]
        to_across(half, b).start()
        rxc[half, b, xl] = acc[half, b, xl, core] + rxc[half, b, xl]

    def sum_chips(half, b):
        to_across(half, b).wait_recv()
        lanes = pl.ds(pl.multiple_of(128 + b * BLOCK, 128), BLOCK)
        img[half, :, lanes] = rxc[half, b, xl] + rxx[half, 0, b]

    def send_edges(half):
        sum_chips(half, 3)

        @pl.when(wide < 31)
        def _():
            to_time(half, 1).start()

        sum_chips(half, 0)

        @pl.when(wide > 0)
        def _():
            to_time(half, 0).start()

    def whiten(half):
        sum_chips(half, 1)
        sum_chips(half, 2)

        @pl.when(wide < 31)
        def _():
            to_time(half, 0).wait_recv()
            img[half, :, rows + 128 :] = halo[half, 0]

        @pl.when(wide == 31)
        def _():
            img[half, :, rows + 128 :] = jnp.zeros((Q, 128), jnp.float32)

        @pl.when(wide > 0)
        def _():
            to_time(half, 1).wait_recv()
            img[half, :, :128] = halo[half, 1]

        @pl.when(wide == 0)
        def _():
            img[half, :, :128] = jnp.zeros((Q, 128), jnp.float32)

        whole = rows + 256
        reps = whole // 128
        spread = lambda ref: jnp.concatenate(
            [jnp.broadcast_to(jnp.concatenate([ref[...]] * 2, axis=1), (32, 128))] * reps, axis=1
        )
        lag_one, lag_two, scale = spread(lag_one_in), spread(lag_two_in), spread(scale_in)
        lane = lax.broadcasted_iota(jnp.int32, (32, whole), 1)
        limit = jnp.where(wide == 31, rows + 128, whole)
        for block in range(Q // 32):
            part = slice(block * 32, block * 32 + 32)
            v = img[half, part, :]
            w = (v - lag_one * pltpu.roll(v, S, 1) - lag_two * pltpu.roll(v, 2 * S, 1)) / scale
            w = jnp.where(lane < limit, w, 0.0)
            ahead, ahead_two = pltpu.roll(w, whole - S, 1), pltpu.roll(w, whole - 2 * S, 1)
            a = (w - lag_one * ahead - lag_two * ahead_two) / scale
            adj[half, mine, part, :] = a[:, 128 : 128 + rows].astype(jnp.bfloat16)
        share(half, 0).start()
        share(half, 1).start()

    def pass_on(half):
        share(half, 0).wait_recv()
        share(half, 2).start()

    def gather(half):
        share(half, 1).wait_recv()
        share(half, 2).wait_recv()

    @pl.loop(0, n_chunks)
    def _(g):
        generate(0, g)

    pl.semaphore_wait(barrier, len(partners))

    @pl.loop(0, 4)
    def _(i):
        b = (i + 3) % 4
        load(b).wait()
        multiply(0, b)

        @pl.when(i > 0)
        def _():
            sum_cores(0, (i + 2) % 4)

    @pl.loop(0, n_chunks)
    def _(g):
        generate(1, g)

        @pl.when(g == 1)
        def _():
            sum_cores(0, 2)

        @pl.when(g == 3)
        def _():
            send_edges(0)

        @pl.when(g == n_chunks - 1)
        def _():
            whiten(0)

    @pl.loop(0, 3)
    def _(i):
        multiply(1, (i + 3) % 4)

        @pl.when(i > 0)
        def _():
            sum_cores(1, (i + 2) % 4)

        @pl.when(i == 1)
        def _():
            pass_on(0)

    gather(0)

    def remote(u, out_sem, in_sem, src, dst, device):
        return pltpu.make_async_remote_copy(
            src, dst, b_send.at[u % 8, out_sem], b_recv.at[u, in_sem],
            device_id=device, device_id_type=MESH,
        )

    def place(color):
        return (y, z) if color == 0 else (z, y)

    def own(color, u, h, j):
        return s_buf.at[u, h, j] if color == 0 else s_buf.at[u, h, :, j]

    def first(color, u, kind):
        d = place(color)[0]
        right, left = rights[color], lefts[color]
        if kind == 0:
            return remote(u, 0, 0, own(color, u, 0, (d + 2) % 4), r1opp.at[u, 0], right)
        if kind == 1:
            return remote(u, 0, 1, own(color, u, 1, (d + 2) % 4), r1opp.at[u, 1], left)
        if kind == 2:
            return remote(u, 0, 2, own(color, u, 1, (d + 1) % 4), r1in.at[u, 0], right)
        if kind == 3:
            return remote(u, 0, 2, own(color, u, 0, (d + 3) % 4), r1in.at[u, 1], left)
        if kind == 4:
            return remote(u, 1, 2, f1.at[u, 0], r1in.at[u, 2], right)
        return remote(u, 1, 2, f1.at[u, 1], r1in.at[u, 3], left)

    def second(color, u, kind):
        d = place(color)[1]
        right, left = rights[1 - color], lefts[1 - color]
        if kind == 0:
            return remote(u, 2, 3, t_b16.at[u, 0, (d + 2) % 4], r2opp.at[u, 0], right)
        if kind == 1:
            return remote(u, 2, 4, t_b16.at[u, 1, (d + 2) % 4], r2opp.at[u, 1], left)
        if kind == 2:
            return remote(u, 2, 5, t_b16.at[u, 1, (d + 1) % 4], r2in.at[u, 0], right)
        if kind == 3:
            return remote(u, 2, 5, t_b16.at[u, 0, (d + 3) % 4], r2in.at[u, 1], left)
        if kind == 4:
            return remote(u, 3, 5, f2.at[u, 0], r2in.at[u, 2], right)
        return remote(u, 3, 5, f2.at[u, 1], r2in.at[u, 3], left)

    def third(u):
        return remote(u, 4, 6, u_b16.at[u], r3.at[u], xmate)

    def all_in(color, u, stage):
        if stage == 0:
            remote(u, 0, 2, r1in.at[u], r1in.at[u], rights[color]).wait_recv()
        else:
            remote(u, 0, 5, r2in.at[u], r2in.at[u], rights[color]).wait_recv()

    def all_out(color, u, out_sem):
        ref = (s_buf.at[u, 0], f1.at[u], t_b16.at[u, 0], f2.at[u])[out_sem]
        remote(u, out_sem, 0, ref, ref, rights[color]).wait_send()

    f32 = lambda v: v.astype(jnp.float32)
    per_half = n_chunks // 2

    def product(n, color):
        u, c = 2 * n + color, 2 * (n % per_half) + color
        lhs = adj[n // per_half].reshape(KH, rows)
        for h in range(2):
            value = jnp.dot(
                lhs, jbuf[:, pl.ds(pl.multiple_of(c * CW + h * HW, HW), HW)], preferred_element_type=jnp.float32
            )
            s_buf[u, h] = value.astype(jnp.bfloat16).reshape(s_buf.shape[2:])
        for kind in range(4):
            first(color, u, kind).start()

    def relay_one(n, color):
        u, d = 2 * n + color, place(color)[0]
        for side in range(2):
            first(color, u, side).wait_recv()
            mine_ref = own(color, u, side, (d + (1 if side == 0 else 3)) % 4)
            f1[u, side] = (f32(r1opp[u, side]) + f32(mine_ref[...])).astype(jnp.bfloat16)
            first(color, u, 4 + side).start()

    def finish_one(n, color):
        u, d = 2 * n + color, place(color)[0]
        all_in(color, u, 0)
        for h in range(2):
            value = f32(own(color, u, h, d)[...]) + f32(r1in[u, 2 + h]) + f32(r1in[u, 1 - h])
            t_f32[u, h] = value
            t_b16[u, h] = value.astype(jnp.bfloat16)
        for kind in range(4):
            second(color, u, kind).start()

    def relay_two(n, color):
        u, d = 2 * n + color, place(color)[1]
        for side in range(2):
            second(color, u, side).wait_recv()
            value = f32(r2opp[u, side]) + t_f32[u, side, (d + (1 if side == 0 else 3)) % 4]
            f2[u, side] = value.astype(jnp.bfloat16)
            second(color, u, 4 + side).start()

    def finish_two(n, color):
        u, d = 2 * n + color, place(color)[1]
        all_in(color, u, 1)
        for h in range(2):
            value = t_f32[u, h, d] + f32(r2in[u, 2 + h]) + f32(r2in[u, 1 - h])
            u_f32[u, h] = value
            u_b16[u, h] = value.astype(jnp.bfloat16)

        @pl.when(n // per_half != xh)
        def _():
            third(u).start()

    def finish(n, color):
        u, c = 2 * n + color, 2 * (n % per_half) + color

        @pl.when(n // per_half == xh)
        def _():
            third(u).wait_recv()
            for h in range(2):
                lanes = pl.ds(pl.multiple_of(c * CW + h * HW, HW), HW)
                out[:, lanes] = u_f32[u, h] + f32(r3[u, h])

    def sent_one(n, color):
        all_out(color, 2 * n + color, 0)

    def sent_two(n, color):
        all_out(color, 2 * n + color, 1)
        all_out(color, 2 * n + color, 2)

    def sent_three(n, color):
        all_out(color, 2 * n + color, 3)

        @pl.when(n // per_half != xh)
        def _():
            third(2 * n + color).wait_send()

    def sent(half):
        for b in range(4):
            to_mate(half, b).wait_send()
            to_across(half, b).wait_send()
        for which in range(3):
            share(half, which).wait_send()

        @pl.when(wide > 0)
        def _():
            to_time(half, 0).wait_send()

        @pl.when(wide < 31)
        def _():
            to_time(half, 1).wait_send()

    stages = (product, relay_one, finish_one, relay_two, finish_two, finish)
    outgoing = ((3, sent_one), (4, sent_two), (5, sent_three))
    n_rounds = 2 * per_half

    @pl.loop(0, n_rounds + len(stages) - 1)
    def _(i):
        for lag, stage in enumerate(stages):

            @pl.when((i >= lag) & (i < n_rounds + lag))
            def _():
                for color in range(2):
                    stage(i - lag, color)

            if lag == 0:

                @pl.when(i == 0)
                def _():
                    multiply(1, 2)
                    sum_cores(1, 1)

                @pl.when(i == per_half - 3)
                def _():
                    sum_cores(1, 2)
                    send_edges(1)

                @pl.when(i == per_half - 2)
                def _():
                    whiten(1)

                @pl.when(i == per_half - 1)
                def _():
                    pass_on(1)
                    gather(1)

        @pl.when((i == per_half) | (i == per_half + 1))
        def _():
            sent(i - per_half)

        for lag, stage in outgoing:

            @pl.when((i >= lag) & (i < n_rounds + lag))
            def _():
                for color in range(2):
                    stage(i - lag, color)


def shards(jacobian, prior_scale, lag_one, lag_two, noise_scale, sketch_seed):
    rows, width = jacobian.shape
    n = width // CW
    bf16, f32 = jnp.bfloat16, jnp.float32
    vmem = pl.BlockSpec(memory_space=pltpu.VMEM)
    product = pl.pallas_call(
        kernel,
        out_shape=jax.ShapeDtypeStruct((K // 32, width), f32),
        in_specs=[
            pl.BlockSpec(memory_space=pl.ANY), vmem, vmem, vmem, vmem,
            pl.BlockSpec(memory_space=pltpu.SMEM),
        ],
        out_specs=vmem,
        scratch_shapes=[
            pltpu.VMEM((rows, width), bf16),
            pltpu.VMEM((KH, width), bf16),
            pltpu.VMEM((2, 4, 2, 2, Q, BLOCK), f32),
            pltpu.VMEM((2, 4, 2, Q, BLOCK), f32),
            pltpu.VMEM((2, 2, 4, Q, BLOCK), f32),
            pltpu.VMEM((2, Q, rows + 256), f32),
            pltpu.VMEM((2, 2, Q, 128), f32),
            pltpu.VMEM((2, 4, Q, rows), bf16),
            pltpu.VMEM((2 * n, 2, 4, 4, 16, HW), bf16),
            pltpu.VMEM((2 * n, 2, 4, 16, HW), bf16),
            pltpu.VMEM((2 * n, 4, 4, 16, HW), bf16),
            pltpu.VMEM((2 * n, 2, 4, 16, HW), bf16),
            pltpu.VMEM((2 * n, 2, 4, 16, HW), f32),
            pltpu.VMEM((2 * n, 2, 4, 16, HW), bf16),
            pltpu.VMEM((2 * n, 2, 16, HW), bf16),
            pltpu.VMEM((2 * n, 4, 16, HW), bf16),
            pltpu.VMEM((2 * n, 2, 16, HW), bf16),
            pltpu.VMEM((2 * n, 2, 16, HW), f32),
            pltpu.VMEM((2 * n, 2, 16, HW), bf16),
            pltpu.VMEM((2 * n, 2, 16, HW), bf16),
            pltpu.SemaphoreType.DMA((4,)),
            pltpu.SemaphoreType.DMA((2, 13)),
            pltpu.SemaphoreType.DMA((2, 13)),
            pltpu.SemaphoreType.DMA((8, 5)),
            pltpu.SemaphoreType.DMA((2 * n, 7)),
        ],
        compiler_params=pltpu.CompilerParams(
            collective_id=0, has_side_effects=True, vmem_limit_bytes=63 * 1024 * 1024
        ),
    )(
        jacobian, prior_scale.reshape(1, width), lag_one.reshape(1, S), lag_two.reshape(1, S),
        noise_scale.reshape(1, S), sketch_seed,
    )
    return product * prior_scale[None, :]


def solution(mesh):
    in_specs = (P("wide", "narrow"), P("narrow"), P(), P(), P(), P())
    out_specs = P("wide", "narrow")
    return jax.shard_map(shards, mesh=mesh, in_specs=in_specs, out_specs=out_specs, check_vma=False)
```

time: 413 us -> 87.8 us (0.21)
  the two profiles are of different devices: /device:TPU:0 before, /device:TPU:12 now
where the time goes in v2:
time: 87.8 us; the launch traced here: 87.5 us
  Pallas kernels  85 us (97%)
  other arithmetic  1.88 us (2%)
    pallas_call x1, Pallas kernels, shards(): pl.pallas_call(kernel, out_shape=jax.ShapeDtypeStruct((K // 32, width), f...  85 us
    mul x1, other arithmetic, shards(): return product * prior_scale[None, :]  1.88 us

profile of v2, /device:TPU:12, one launch (start us, length us, event | category | flops | bytes accessed | tf_op | source)
XLA Modules:
  0.0 87.5 jit_solution(902502434999956290)
XLA Ops:
  0.0 0.0 copy-start
  0.7 85.0 %shard_map.64 = f32[16,8192]{1,0:T(8,128)} custom-call(bf16[1024,8192]{1,0:T(8,128)(2,1)} %j_hbm.1, f32[1,8192]{1,0:T(1,128)} %bitcast.4, f32[1,64]{1,0:T(1,128)} %bitcast.5, f32[1,64]{1,0:T(1,128)} %bitcast.6, f32[1,64]{1,0:T(1,128)} %bitcast.7, s32[1]{0:T(128)S(6)} %copy.7.seed), custom_call_target="tpu_custom_call" | custom-call | tf_op jit(solution)/shard_map/pallas_call | solution.py:433
  85.6 0.0 copy-done
  85.6 1.9 %broadcast_multiply_fusion = f32[16,8192]{1,0:T(8,128)} fusion(f32[16,8192]{1,0:T(8,128)} %shard_map.64, f32[8192]{0:T(1024)S(1)} %copy-done), kind=kLoop, calls=%fused_computation | loop fusion | flops 131072 | bytes 1081344 | tf_op jit(solution)/shard_map/mul | solution.py:475
Async XLA Ops:
  0.0 85.6 %copy-start = (f32[8192]{0:T(1024)S(1)}, f32[8192]{0:T(1024)}, u32[]{:S(2)}) copy-start(f32[8192]{0:T(1024)} %param.7) | copy-start | bytes 98308

commit v3 on v2

--- a/solution.py
+++ b/solution.py
@@ -11,7 +11,10 @@
 K = 512
 S = 64
 MESH = pl.DeviceIdType.MESH
-CW = 1024
+GW = 1024
+CW = 512
+FINALS = 1
+SLOTS = 8
 HW = CW // 2
 BLOCK = 256
 KH = K // 2
@@ -23,8 +26,8 @@
 def kernel(
     j_hbm, prior, lag_one_in, lag_two_in, scale_in, seed, out,
     jbuf, sk, acc, rxc, rxx, img, halo, adj,
-    s_buf, r1opp, r1in, f1, t_f32, t_b16, r2opp, r2in, f2, u_f32, u_b16, r3,
-    j_sem, a_send, a_recv, b_send, b_recv,
+    s_buf, r1opp, r1in, f1, t_f32, t_b16, r2opp, r2in, f2, u_f32, u_b16, r3, x_out, x_in,
+    j_sem, a_send, a_recv, b_send, b_recv, x_send, x_recv,
 ):
     rows, width = jbuf.shape
     n_chunks = width // CW
@@ -55,16 +58,16 @@
     salt_high, salt_low = salt & -512, salt & 511
 
     def generate(half, g):
-        first = narrow * width + g * CW
-        lanes = pl.ds(pl.multiple_of(g * CW, CW), CW)
+        first = narrow * width + g * GW
+        lanes = pl.ds(pl.multiple_of(g * GW, GW), GW)
         across_p = (
-            ((lax.broadcasted_iota(jnp.int32, (16, CW), 1) + first) * 512) ^ salt_high
+            ((lax.broadcasted_iota(jnp.int32, (16, GW), 1) + first) * 512) ^ salt_high
         ) * M1
-        scale = jnp.broadcast_to(prior[:, lanes] * SPREAD, (16, CW))
+        scale = jnp.broadcast_to(prior[:, lanes] * SPREAD, (16, GW))
         for block in range(KH // 16):
             down = lax.broadcasted_iota(jnp.int32, (16, 128), 0) + (half * KH + block * 16)
             down = (down ^ salt_low) * M1
-            h = across_p + jnp.concatenate([down] * (CW // 128), axis=1)
+            h = across_p + jnp.concatenate([down] * (GW // 128), axis=1)
             h = h ^ lax.shift_right_logical(h, 15)
             h = h * M2
             h = h ^ lax.shift_right_logical(h, 12)
@@ -86,14 +89,14 @@
     def to_mate(half, b):
         return pltpu.make_async_remote_copy(
             acc.at[half, b, :, 1 - core], rxc.at[half, b],
-            a_send.at[half, b], a_recv.at[half, b],
+            a_send.at[0], a_recv.at[half, b],
             device_id=mate, device_id_type=MESH,
         )
 
     def to_across(half, b):
         return pltpu.make_async_remote_copy(
             rxx.at[half, 1, b], rxx.at[half, 0, b],
-            a_send.at[half, 4 + b], a_recv.at[half, 4 + b],
+            a_send.at[1], a_recv.at[half, 4 + b],
             device_id=across, device_id_type=MESH,
         )
 
@@ -101,7 +104,7 @@
         low = 128 if side == 0 else rows
         return pltpu.make_async_remote_copy(
             img.at[half, :, low : low + 128], halo.at[half, side],
-            a_send.at[half, 8 + side], a_recv.at[half, 8 + side],
+            a_send.at[3 + side], a_recv.at[half, 8 + side],
             device_id=earlier if side == 0 else later, device_id_type=MESH,
         )
 
@@ -110,7 +113,7 @@
     def share(half, which):
         q = mine if which < 2 else (1 - xl) * 2 + core
         return pltpu.make_async_remote_copy(
-            adj.at[half, q], adj.at[half, q], a_send.at[half, 10 + which], a_recv.at[half, 10 + which],
+            adj.at[half, q], adj.at[half, q], a_send.at[2], a_recv.at[half, 10 + which],
             device_id=across if which == 0 else mate, device_id_type=MESH,
         )
 
@@ -187,7 +190,7 @@
         share(half, 1).wait_recv()
         share(half, 2).wait_recv()
 
-    @pl.loop(0, n_chunks)
+    @pl.loop(0, width // GW)
     def _(g):
         generate(0, g)
 
@@ -203,7 +206,7 @@
         def _():
             sum_cores(0, (i + 2) % 4)
 
-    @pl.loop(0, n_chunks)
+    @pl.loop(0, width // GW)
     def _(g):
         generate(1, g)
 
@@ -215,7 +218,7 @@
         def _():
             send_edges(0)
 
-        @pl.when(g == n_chunks - 1)
+        @pl.when(g == width // GW - 1)
         def _():
             whiten(0)
 
@@ -233,9 +236,12 @@
 
     gather(0)
 
+    per_half = n_chunks // 2 - FINALS
+    final = 2 * per_half
+
     def remote(u, out_sem, in_sem, src, dst, device):
         return pltpu.make_async_remote_copy(
-            src, dst, b_send.at[u % 8, out_sem], b_recv.at[u, in_sem],
+            src, dst, b_send.at[out_sem], b_recv.at[u % (2 * SLOTS), in_sem],
             device_id=device, device_id_type=MESH,
         )
 
@@ -251,68 +257,87 @@
         if kind == 0:
             return remote(u, 0, 0, own(color, u, 0, (d + 2) % 4), r1opp.at[u, 0], right)
         if kind == 1:
-            return remote(u, 0, 1, own(color, u, 1, (d + 2) % 4), r1opp.at[u, 1], left)
+            return remote(u, 0, 0, own(color, u, 1, (d + 2) % 4), r1opp.at[u, 1], left)
         if kind == 2:
-            return remote(u, 0, 2, own(color, u, 1, (d + 1) % 4), r1in.at[u, 0], right)
+            return remote(u, 0, 1, own(color, u, 1, (d + 1) % 4), r1in.at[u, 0], right)
         if kind == 3:
-            return remote(u, 0, 2, own(color, u, 0, (d + 3) % 4), r1in.at[u, 1], left)
+            return remote(u, 0, 1, own(color, u, 0, (d + 3) % 4), r1in.at[u, 1], left)
         if kind == 4:
-            return remote(u, 1, 2, f1.at[u, 0], r1in.at[u, 2], right)
-        return remote(u, 1, 2, f1.at[u, 1], r1in.at[u, 3], left)
+            return remote(u, 1, 1, f1.at[u, 0], r1in.at[u, 2], right)
+        return remote(u, 1, 1, f1.at[u, 1], r1in.at[u, 3], left)
 
     def second(color, u, kind):
         d = place(color)[1]
         right, left = rights[1 - color], lefts[1 - color]
         if kind == 0:
-            return remote(u, 2, 3, t_b16.at[u, 0, (d + 2) % 4], r2opp.at[u, 0], right)
+            return remote(u, 2, 2, t_b16.at[u, 0, (d + 2) % 4], r2opp.at[u, 0], right)
         if kind == 1:
-            return remote(u, 2, 4, t_b16.at[u, 1, (d + 2) % 4], r2opp.at[u, 1], left)
+            return remote(u, 2, 2, t_b16.at[u, 1, (d + 2) % 4], r2opp.at[u, 1], left)
         if kind == 2:
-            return remote(u, 2, 5, t_b16.at[u, 1, (d + 1) % 4], r2in.at[u, 0], right)
+            return remote(u, 2, 3, t_b16.at[u, 1, (d + 1) % 4], r2in.at[u, 0], right)
         if kind == 3:
-            return remote(u, 2, 5, t_b16.at[u, 0, (d + 3) % 4], r2in.at[u, 1], left)
+            return remote(u, 2, 3, t_b16.at[u, 0, (d + 3) % 4], r2in.at[u, 1], left)
         if kind == 4:
-            return remote(u, 3, 5, f2.at[u, 0], r2in.at[u, 2], right)
-        return remote(u, 3, 5, f2.at[u, 1], r2in.at[u, 3], left)
+            return remote(u, 3, 3, f2.at[u, 0], r2in.at[u, 2], right)
+        return remote(u, 3, 3, f2.at[u, 1], r2in.at[u, 3], left)
 
     def third(u):
-        return remote(u, 4, 6, u_b16.at[u], r3.at[u], xmate)
-
-    def all_in(color, u, stage):
-        if stage == 0:
-            remote(u, 0, 2, r1in.at[u], r1in.at[u], rights[color]).wait_recv()
-        else:
-            remote(u, 0, 5, r2in.at[u], r2in.at[u], rights[color]).wait_recv()
-
-    def all_out(color, u, out_sem):
-        ref = (s_buf.at[u, 0], f1.at[u], t_b16.at[u, 0], f2.at[u])[out_sem]
-        remote(u, out_sem, 0, ref, ref, rights[color]).wait_send()
+        return pltpu.make_async_remote_copy(
+            u_b16.at[u], r3.at[u], x_send.at[0], x_recv.at[0],
+            device_id=xmate, device_id_type=MESH,
+        )
+
+    def all_in(color, u, in_sem):
+        ref = (r1opp, r1in, r2opp, r2in)[in_sem].at[u]
+        remote(u, 0, in_sem, ref, ref, rights[color]).wait_recv()
 
     f32 = lambda v: v.astype(jnp.float32)
-    per_half = n_chunks // 2
+    def terms(half, c, h):
+        lanes = pl.ds(pl.multiple_of(c * CW + h * HW, HW), HW)
+        return jnp.dot(
+            adj[half].reshape(KH, rows), jbuf[:, lanes], preferred_element_type=jnp.float32
+        )
+
+    def to_x(e):
+        return pltpu.make_async_remote_copy(
+            x_out.at[e], x_in.at[e], x_send.at[1], x_recv.at[1 + e],
+            device_id=xmate, device_id_type=MESH,
+        )
+
+    def exchange(e):
+        for h in range(2):
+            value = terms(1 - xh, final + e, h)
+            x_out[e, h] = value.astype(jnp.bfloat16).reshape(x_out.shape[2:])
+        to_x(e).start()
 
     def product(n, color):
         u, c = 2 * n + color, 2 * (n % per_half) + color
-        lhs = adj[n // per_half].reshape(KH, rows)
         for h in range(2):
-            value = jnp.dot(
-                lhs, jbuf[:, pl.ds(pl.multiple_of(c * CW + h * HW, HW), HW)], preferred_element_type=jnp.float32
-            )
+            value = terms(n // per_half, c, h)
             s_buf[u, h] = value.astype(jnp.bfloat16).reshape(s_buf.shape[2:])
         for kind in range(4):
             first(color, u, kind).start()
 
+    def product_final(n, color):
+        u, e = 2 * n + color, 2 * (n - final) + color
+        to_x(e).wait_recv()
+        for h in range(2):
+            value = terms(xh, final + e, h).reshape(s_buf.shape[2:]) + f32(x_in[e, h])
+            s_buf[u, h] = value.astype(jnp.bfloat16)
+        for kind in range(4):
+            first(color, u, kind).start()
+
     def relay_one(n, color):
         u, d = 2 * n + color, place(color)[0]
+        all_in(color, u, 0)
         for side in range(2):
-            first(color, u, side).wait_recv()
             mine_ref = own(color, u, side, (d + (1 if side == 0 else 3)) % 4)
             f1[u, side] = (f32(r1opp[u, side]) + f32(mine_ref[...])).astype(jnp.bfloat16)
             first(color, u, 4 + side).start()
 
     def finish_one(n, color):
         u, d = 2 * n + color, place(color)[0]
-        all_in(color, u, 0)
+        all_in(color, u, 1)
         for h in range(2):
             value = f32(own(color, u, h, d)[...]) + f32(r1in[u, 2 + h]) + f32(r1in[u, 1 - h])
             t_f32[u, h] = value
@@ -322,112 +347,124 @@
 
     def relay_two(n, color):
         u, d = 2 * n + color, place(color)[1]
+        all_in(color, u, 2)
         for side in range(2):
-            second(color, u, side).wait_recv()
             value = f32(r2opp[u, side]) + t_f32[u, side, (d + (1 if side == 0 else 3)) % 4]
             f2[u, side] = value.astype(jnp.bfloat16)
             second(color, u, 4 + side).start()
 
     def finish_two(n, color):
         u, d = 2 * n + color, place(color)[1]
-        all_in(color, u, 1)
+        all_in(color, u, 3)
         for h in range(2):
             value = t_f32[u, h, d] + f32(r2in[u, 2 + h]) + f32(r2in[u, 1 - h])
             u_f32[u, h] = value
             u_b16[u, h] = value.astype(jnp.bfloat16)
 
-        @pl.when(n // per_half != xh)
+        @pl.when((n < final) & (n // per_half != xh))
         def _():
             third(u).start()
 
-    def finish(n, color):
-        u, c = 2 * n + color, 2 * (n % per_half) + color
-
-        @pl.when(n // per_half == xh)
-        def _():
-            third(u).wait_recv()
+        @pl.when(n >= final)
+        def _():
+            c = final + 2 * (n - final) + color
             for h in range(2):
-                lanes = pl.ds(pl.multiple_of(c * CW + h * HW, HW), HW)
-                out[:, lanes] = u_f32[u, h] + f32(r3[u, h])
-
-    def sent_one(n, color):
-        all_out(color, 2 * n + color, 0)
-
-    def sent_two(n, color):
-        all_out(color, 2 * n + color, 1)
-        all_out(color, 2 * n + color, 2)
-
-    def sent_three(n, color):
-        all_out(color, 2 * n + color, 3)
-
-        @pl.when(n // per_half != xh)
-        def _():
-            third(2 * n + color).wait_send()
-
-    def sent(half):
-        for b in range(4):
-            to_mate(half, b).wait_send()
-            to_across(half, b).wait_send()
-        for which in range(3):
-            share(half, which).wait_send()
-
-        @pl.when(wide > 0)
-        def _():
-            to_time(half, 0).wait_send()
-
-        @pl.when(wide < 31)
-        def _():
-            to_time(half, 1).wait_send()
-
-    stages = (product, relay_one, finish_one, relay_two, finish_two, finish)
-    outgoing = ((3, sent_one), (4, sent_two), (5, sent_three))
-    n_rounds = 2 * per_half
-
-    @pl.loop(0, n_rounds + len(stages) - 1)
+                out[:, pl.ds(pl.multiple_of(c * CW + h * HW, HW), HW)] = u_f32[u, h]
+
+    def collect():
+        ref = r3.at[pl.ds(xh * final, final)]
+        pltpu.make_async_remote_copy(
+            ref, ref, x_send.at[0], x_recv.at[0], device_id=xmate, device_id_type=MESH
+        ).wait_recv()
+
+        for c in range(final):
+            u = xh * final + c
+            for h in range(2):
+                low = c * CW + h * HW
+                out[:, low : low + HW] = u_f32[u, h] + f32(r3[u, h])
+
+        ref = u_b16.at[pl.ds((1 - xh) * final, final)]
+        pltpu.make_async_remote_copy(
+            ref, ref, x_send.at[0], x_recv.at[0], device_id=xmate, device_id_type=MESH
+        ).wait_send()
+
+    def leave(src, sem):
+        pltpu.make_async_remote_copy(
+            src, src, sem, a_recv.at[0, 0], device_id=mate, device_id_type=MESH
+        ).wait_send()
+
+    stages = ((0, product), (2, relay_one), (4, finish_one), (6, relay_two), (8, finish_two))
+    n_rounds = final + FINALS
+
+    @pl.loop(0, n_rounds + 8)
     def _(i):
-        for lag, stage in enumerate(stages):
-
-            @pl.when((i >= lag) & (i < n_rounds + lag))
+        @pl.when(i == per_half)
+        def _():
+            gather(1)
+
+        for lag, stage in stages:
+
+            @pl.when((i >= lag) & (i < (final if lag == 0 else n_rounds + lag)))
             def _():
                 for color in range(2):
                     stage(i - lag, color)
 
             if lag == 0:
+
+                @pl.when((i >= final) & (i < n_rounds))
+                def _():
+                    for color in range(2):
+                        product_final(i, color)
 
                 @pl.when(i == 0)
                 def _():
                     multiply(1, 2)
                     sum_cores(1, 1)
-
-                @pl.when(i == per_half - 3)
+                    send_edges(1)
+
+                @pl.when(i == 1)
                 def _():
                     sum_cores(1, 2)
-                    send_edges(1)
+
+                @pl.when(i == per_half - 4)
+                def _():
+                    whiten(1)
 
                 @pl.when(i == per_half - 2)
                 def _():
-                    whiten(1)
-
-                @pl.when(i == per_half - 1)
+                    pass_on(1)
+
+                started = i - (per_half - 4) - (1 - xh) * 4
+
+                @pl.when((started >= 0) & (started < 2 * FINALS))
                 def _():
-                    pass_on(1)
-                    gather(1)
-
-        @pl.when((i == per_half) | (i == per_half + 1))
-        def _():
-            sent(i - per_half)
-
-        for lag, stage in outgoing:
-
-            @pl.when((i >= lag) & (i < n_rounds + lag))
-            def _():
-                for color in range(2):
-                    stage(i - lag, color)
+                    exchange(started)
+
+    collect()
+
+    leave(acc.at[:, :, :, 1 - core], a_send.at[0])
+    leave(rxx.at[:, 1], a_send.at[1])
+    leave(adj.at[:, 0:3], a_send.at[2])
+
+    @pl.when(wide > 0)
+    def _():
+        leave(halo.at[:, 0], a_send.at[3])
+
+    @pl.when(wide < 31)
+    def _():
+        leave(halo.at[:, 1], a_send.at[4])
+
+    leave(s_buf.at[:, 0], b_send.at[0])
+    leave(f1, b_send.at[1])
+    leave(t_b16.at[:, 0], b_send.at[2])
+    leave(f2, b_send.at[3])
+    leave(x_out, x_send.at[1])
 
 
 def shards(jacobian, prior_scale, lag_one, lag_two, noise_scale, sketch_seed):
     rows, width = jacobian.shape
     n = width // CW
+    units = 2 * (n - FINALS)
     bf16, f32 = jnp.bfloat16, jnp.float32
     vmem = pl.BlockSpec(memory_space=pltpu.VMEM)
     product = pl.pallas_call(
@@ -447,23 +484,27 @@
             pltpu.VMEM((2, Q, rows + 256), f32),
             pltpu.VMEM((2, 2, Q, 128), f32),
             pltpu.VMEM((2, 4, Q, rows), bf16),
-            pltpu.VMEM((2 * n, 2, 4, 4, 16, HW), bf16),
-            pltpu.VMEM((2 * n, 2, 4, 16, HW), bf16),
-            pltpu.VMEM((2 * n, 4, 4, 16, HW), bf16),
-            pltpu.VMEM((2 * n, 2, 4, 16, HW), bf16),
-            pltpu.VMEM((2 * n, 2, 4, 16, HW), f32),
-            pltpu.VMEM((2 * n, 2, 4, 16, HW), bf16),
-            pltpu.VMEM((2 * n, 2, 16, HW), bf16),
-            pltpu.VMEM((2 * n, 4, 16, HW), bf16),
-            pltpu.VMEM((2 * n, 2, 16, HW), bf16),
-            pltpu.VMEM((2 * n, 2, 16, HW), f32),
-            pltpu.VMEM((2 * n, 2, 16, HW), bf16),
-            pltpu.VMEM((2 * n, 2, 16, HW), bf16),
+            pltpu.VMEM((units, 2, 4, 4, 16, HW), bf16),
+            pltpu.VMEM((units, 2, 4, 16, HW), bf16),
+            pltpu.VMEM((units, 4, 4, 16, HW), bf16),
+            pltpu.VMEM((units, 2, 4, 16, HW), bf16),
+            pltpu.VMEM((units, 2, 4, 16, HW), f32),
+            pltpu.VMEM((units, 2, 4, 16, HW), bf16),
+            pltpu.VMEM((units, 2, 16, HW), bf16),
+            pltpu.VMEM((units, 4, 16, HW), bf16),
+            pltpu.VMEM((units, 2, 16, HW), bf16),
+            pltpu.VMEM((units, 2, 16, HW), f32),
+            pltpu.VMEM((units, 2, 16, HW), bf16),
+            pltpu.VMEM((units, 2, 16, HW), bf16),
+            pltpu.VMEM((2 * FINALS, 2, 4, 4, 16, HW), bf16),
+            pltpu.VMEM((2 * FINALS, 2, 4, 4, 16, HW), bf16),
             pltpu.SemaphoreType.DMA((4,)),
+            pltpu.SemaphoreType.DMA((5,)),
             pltpu.SemaphoreType.DMA((2, 13)),
-            pltpu.SemaphoreType.DMA((2, 13)),
-            pltpu.SemaphoreType.DMA((8, 5)),
-            pltpu.SemaphoreType.DMA((2 * n, 7)),
+            pltpu.SemaphoreType.DMA((4,)),
+            pltpu.SemaphoreType.DMA((2 * SLOTS, 4)),
+            pltpu.SemaphoreType.DMA((2,)),
+            pltpu.SemaphoreType.DMA((1 + 2 * FINALS,)),
         ],
         compiler_params=pltpu.CompilerParams(
             collective_id=0, has_side_effects=True, vmem_limit_bytes=63 * 1024 * 1024

time: 87.8 us -> 85.1 us (0.969)
  the two profiles are of different devices: /device:TPU:12 before, /device:TPU:0 now
where the time goes in v3:
time: 85.1 us; the launch traced here: 84.8 us
  Pallas kernels  82.3 us (97%)
  other arithmetic  1.88 us (2%)
    pallas_call x1, Pallas kernels, shards(): pl.pallas_call(kernel, out_shape=jax.ShapeDtypeStruct((K // 32, width), f...  82.3 us
    mul x1, other arithmetic, shards(): return product * prior_scale[None, :]  1.88 us

profile of v3, /device:TPU:0, one launch (start us, length us, event | category | flops | bytes accessed | tf_op | source)
XLA Modules:
  0.0 84.8 jit_solution(14829608947129848812)
XLA Ops:
  0.0 0.0 copy-start
  0.7 82.3 %shard_map.64 = f32[16,8192]{1,0:T(8,128)} custom-call(bf16[1024,8192]{1,0:T(8,128)(2,1)} %j_hbm.1, f32[1,8192]{1,0:T(1,128)} %bitcast.4, f32[1,64]{1,0:T(1,128)} %bitcast.5, f32[1,64]{1,0:T(1,128)} %bitcast.6, f32[1,64]{1,0:T(1,128)} %bitcast.7, s32[1]{0:T(128)S(6)} %copy.7.seed), custom_call_target="tpu_custom_call" | custom-call | tf_op jit(solution)/shard_map/pallas_call | solution.py:470
  83.0 0.0 copy-done
  83.0 1.9 %broadcast_multiply_fusion = f32[16,8192]{1,0:T(8,128)} fusion(f32[16,8192]{1,0:T(8,128)} %shard_map.64, f32[8192]{0:T(1024)S(1)} %copy-done), kind=kLoop, calls=%fused_computation | loop fusion | flops 131072 | bytes 1081344 | tf_op jit(solution)/shard_map/mul | solution.py:516
Async XLA Ops:
  0.0 83.0 %copy-start = (f32[8192]{0:T(1024)S(1)}, f32[8192]{0:T(1024)}, u32[]{:S(2)}) copy-start(f32[8192]{0:T(1024)} %param.7) | copy-start | bytes 98308
